TPU v7x, 512 devices: a whole 4x4x16 slice. The times are simulated.
512 devices in a mesh: dp: 8 (over x, y_lo), tm: 64 (over z, y_hi, core).
Axes of the slice: x: 4, y: 4 (y_hi: 2, y_lo: 2; y = y_hi * 2 + y_lo), z: 16, core: 2. Of those that a mesh axis runs over, the one named last changes fastest.
Arguments:
- features: bfloat16 [8, 8192, 1536], P('dp', 'tm'), may hold values from -8 to 8
- start_noise: bfloat16 [8, 8192, 1536], P('dp', 'tm'), may hold values from -1 to 1
- cotangent: bfloat16 [8, 8192, 1536], P('dp', 'tm'), may hold values from -0.0234375 to 0.0234375
- in_weight: bfloat16 [3072, 1536], P('tm'), may hold values from -0.15625 to 0.15625
- kernel: float32 [31, 1536], replicated, may hold values from -1 to 1
- bn_gain: float32 [1536], replicated, may hold values from 0.25 to 1.75
- bn_shift: float32 [1536], replicated, may hold values from -1 to 1
- ends: int32 [8], replicated, may hold values from 4096 to 8192
Outputs:
- perturbation: float32 [8, 8192, 1536], P('dp', 'tm')
- grad_kernel: float32 [31, 1536], P(None, 'tm')
- grad_norm: float32 [2, 1536], P(None, 'tm')
Inputs may be any that keep to these rules, and one draw needn't show every extreme that they name: `ends`: frames at or after an utterance's end are padding.
All inputs are finite; a program needn't handle non-finite values.
Results may differ from a plain program's by a relative error of at most 0.0059.
Values may be sent and summed in bfloat16 or wider, within the bound.
A program may use at most 128 MiB of HBM per device.

v0:
```python
import jax
import jax.numpy as jnp
from jax import lax
from jax.sharding import PartitionSpec as P

ASCENT = 2
noise_scale = 0.5
ascent_rate = 0.5
layer_epsilon = 1e-05
batch_epsilon = 1e-05
ascent_epsilon = 1e-06


def normalize(summed):
    centre = summed - jnp.mean(summed, axis=-1, keepdims=True)
    inverse = lax.rsqrt(jnp.mean(centre * centre, axis=-1, keepdims=True) + layer_epsilon)
    return (centre * inverse, inverse)


def with_halo(block, half_span):
    count = lax.axis_size("tm")
    before = lax.ppermute(block[-half_span:], "tm", [(i, i + 1) for i in range(count - 1)])
    after = lax.ppermute(block[:half_span], "tm", [(i + 1, i) for i in range(count - 1)])
    return jnp.concatenate([before, block, after], axis=0).astype(jnp.float32)


def conv(padded, kernel, out_length, flip):
    taps = kernel.shape[0]
    result = None
    for offset in range(taps):
        start = taps - 1 - offset if flip else offset
        term = kernel[offset] * padded[start : start + out_length]
        result = term if result is None else result + term
    return result


def tap_grad(grad, padded, taps):
    rows = grad.shape[0]
    return jnp.stack([jnp.sum(grad * padded[j : j + rows], axis=0) for j in range(taps)])


def on_device(features, start_noise, cotangent, in_weight, kernel, bn_gain, bn_shift, ends):
    frame_rows = features.shape[1]
    model_width = features.shape[2]
    tap_count = kernel.shape[0]
    half_span = (tap_count - 1) // 2
    shard_index = lax.axis_index("tm")
    group_index = lax.axis_index("dp")
    utter_end = lax.dynamic_index_in_dim(ends, group_index, 0, keepdims=False)
    live_count = jnp.sum(ends).astype(jnp.float32)
    utter_length = utter_end.astype(jnp.float32)
    frame_ids = shard_index * frame_rows + jnp.arange(frame_rows, dtype=jnp.int32)
    live = (frame_ids < utter_end).astype(jnp.float32)[:, None]
    weight_full = lax.all_gather(in_weight, "tm", axis=0, tiled=True)
    inputs = features[0].astype(jnp.float32)
    perturbation = noise_scale * start_noise[0].astype(jnp.float32) * live
    upstream = live * cotangent[0].astype(jnp.float32) / ASCENT
    everywhere = ("dp", "tm")
    kernel_part = 0.0
    norm_part = 0.0
    for ascent_step in range(ASCENT):
        summed = inputs + perturbation
        normed, inverse = normalize(summed)
        hidden = lax.dot_general(
            normed.astype(jnp.bfloat16),
            weight_full,
            (((1,), (1,)), ((), ())),
            preferred_element_type=jnp.float32,
        )
        value_half = hidden[:, :model_width]
        gate_half = jax.nn.sigmoid(hidden[:, model_width:])
        glu = (value_half * gate_half * live).astype(jnp.bfloat16)
        padded = with_halo(glu, half_span)
        conv_out = conv(padded, kernel, frame_rows, False)
        batch_mean = lax.psum(jnp.sum(live * conv_out, axis=0), everywhere) / live_count
        centred = conv_out - batch_mean
        variance = lax.psum(jnp.sum(live * centred * centred, axis=0), everywhere) / live_count
        inv_std = lax.rsqrt(variance + batch_epsilon)
        scaled = centred * inv_std
        pre_act = bn_gain * scaled + bn_shift
        pre_sigmoid = jax.nn.sigmoid(pre_act)
        grad_pre = upstream * pre_sigmoid * (1.0 + pre_act * (1.0 - pre_sigmoid))
        both = lax.psum(
            jnp.stack([jnp.sum(grad_pre * scaled, axis=0), jnp.sum(grad_pre, axis=0)]), everywhere
        )
        norm_part = norm_part + both
        grad_conv = (
            live * inv_std * bn_gain * (grad_pre - (both[1] + scaled * both[0]) / live_count)
        ).astype(jnp.bfloat16)
        kernel_part = kernel_part + tap_grad(grad_conv.astype(jnp.float32), padded, tap_count)
        if ascent_step + 1 < ASCENT:
            grad_pad = with_halo(grad_conv, half_span)
            grad_glu = (conv(grad_pad, kernel, frame_rows, True) * live).astype(jnp.bfloat16)
            grad_float = grad_glu.astype(jnp.float32)
            grad_hidden = jnp.concatenate(
                [grad_float * gate_half, grad_float * value_half * gate_half * (1.0 - gate_half)],
                axis=1,
            ).astype(jnp.bfloat16)
            grad_normed = jnp.dot(grad_hidden, weight_full, preferred_element_type=jnp.float32)
            direction = (
                live
                * inverse
                * (
                    grad_normed
                    - jnp.mean(grad_normed, axis=-1, keepdims=True)
                    - normed * jnp.mean(grad_normed * normed, axis=-1, keepdims=True)
                )
            )
            square_total = lax.psum(jnp.sum(direction * direction), "tm")
            perturbation = perturbation + direction * (
                ascent_rate
                * jnp.sqrt(utter_length * model_width)
                / (jnp.sqrt(square_total) + ascent_epsilon)
            )
    width = model_width // lax.axis_size("tm")
    by_shard = jnp.transpose(kernel_part.reshape(tap_count, -1, width), (1, 0, 2))
    by_shard = jnp.pad(by_shard.reshape(by_shard.shape[0], -1), ((0, 0), (0, 24)))
    kernel_total = lax.psum_scatter(by_shard.reshape(-1, 6, 128), "tm", scatter_dimension=0)
    kernel_total = lax.psum(kernel_total, "dp").reshape(-1)[: tap_count * width]
    kernel_total = kernel_total.reshape(tap_count, width)
    norm_total = lax.dynamic_slice_in_dim(norm_part, shard_index * width, width, 1)
    return (perturbation[None], kernel_total, norm_total)


def solution(mesh):
    return jax.shard_map(
        on_device,
        mesh=mesh,
        in_specs=(
            P("dp", "tm", None),
            P("dp", "tm", None),
            P("dp", "tm", None),
            P("tm", None),
            P(),
            P(),
            P(),
            P(),
        ),
        out_specs=(P("dp", "tm", None), P(None, "tm"), P(None, "tm")),
        check_vma=False,
    )
```

profile of v0, /device:TPU:2, one launch (start us, length us, event | category | flops | bytes accessed | tf_op | source)
XLA Modules:
  0.0 1536.4 jit_solution(2124826723035073364)
XLA Ops:
  7.2 0.7 all-gather.2.cloned.1.call-update
  8.0 1.2 dynamic_slice.7
  10.6 1.7 slice_reduce_fusion.34
  12.3 1.4 fusion.121
  13.7 1.4 multiply_reduce_fusion.7
  15.1 1.2 broadcast_select_fusion
  16.3 168.6 %all-gather.2.cloned.1.call-done = bf16[3072,1536]{1,0:T(8,128)(2,1)} async-done(((bf16[48,1536]{1,0:T(8,128)(2,1)}), bf16[3072,1536]{1,0:T(8,128)(2,1)}) %all-gather.2.cloned.1.call-update) | async-done | bytes 9437200 | tf_op jit(solution)/shard_map/all_gather | solution.py:54
  184.9 6.9 fusion.122
  192.1 2.2 collective-permute-start
  194.3 1.3 collective-permute-start.1
  195.6 2.0 slice_reduce_fusion.33
  199.8 4.6 multiply_reduce_fusion.6
  204.3 104.9 %psum.56 = f32[1536]{0:T(1024)} all-reduce(f32[1536]{0:T(1024)} %get-tuple-element.124), channel_id=1, replica_groups=mesh['dp'=8,'tm'=64] {'dp','tm'}, use_global_device_ids=true, to_apply=%region_3.4 | all-reduce | flops 1536 | bytes 12288 | tf_op jit(solution)/shard_map/psum | solution.py:75
  309.2 0.7 broadcast_divide_fusion.1
  309.9 1.4 fusion.4
  311.3 99.4 %psum.57 = f32[1536]{0:T(1024)} all-reduce(f32[1536]{0:T(1024)} %fusion.4), channel_id=1, replica_groups=mesh['dp'=8,'tm'=64] {'dp','tm'}, use_global_device_ids=true, to_apply=%region_6.7 | all-reduce | flops 1536 | bytes 12288 | tf_op jit(solution)/shard_map/psum | solution.py:77
  410.7 0.7 add_rsqrt_fusion.1
  412.0 2.4 multiply_reduce_fusion.5
  415.0 100.9 %psum.58 = f32[2,1536]{1,0:T(2,128)} all-reduce(f32[2,1536]{1,0:T(2,128)} %pad_maximum_fusion), channel_id=1, replica_groups=mesh['dp'=8,'tm'=64] {'dp','tm'}, use_global_device_ids=true, to_apply=%region_9.10 | all-reduce | flops 3072 | bytes 24576 | tf_op jit(solution)/shard_map/psum | solution.py:83
  515.9 0.8 slice_reduce_fusion.3
  516.7 4.1 fusion.36
  520.9 1.2 fusion.35
  527.2 1.8 collective-permute-start.2
  528.9 1.3 collective-permute-start.3
  530.7 3.2 collective-permute-done.3
  534.2 3.2 fusion
  537.8 0.7 copy-done.1
  538.7 1.5 fusion.134
  540.2 1.2 multiply_reduce_fusion.3
  541.4 133.6 %psum.59 = f32[]{:T(128)} all-reduce(f32[]{:T(128)} %get-tuple-element.119), channel_id=1, replica_groups=mesh['dp'=8,'tm'=64] {'tm'}, use_global_device_ids=true, to_apply=%region_13.14 | all-reduce | flops 1 | bytes 8 | tf_op jit(solution)/shard_map/psum | solution.py:109
  675.7 1.1 fusion.136
  677.1 6.8 fusion.124
  684.2 1.3 collective-permute-start.4
  685.5 1.5 collective-permute-start.5
  687.1 1.6 collective-permute-done.5
  688.8 3.1 multiply_reduce_fusion.1
  692.0 114.4 %psum.60 = f32[1536]{0:T(1024)S(1)} all-reduce(f32[1536]{0:T(1024)S(1)} %get-tuple-element.114), channel_id=1, replica_groups=mesh['dp'=8,'tm'=64] {'dp','tm'}, use_global_device_ids=true, to_apply=%region_48.49 | all-reduce | flops 1536 | bytes 12288 | tf_op jit(solution)/shard_map/psum | solution.py:75
  806.6 99.4 %psum.61 = f32[1536]{0:T(1024)S(1)} all-reduce(f32[1536]{0:T(1024)S(1)} %fusion.5), channel_id=1, replica_groups=mesh['dp'=8,'tm'=64] {'dp','tm'}, use_global_device_ids=true, to_apply=%region_50.51 | all-reduce | flops 1536 | bytes 12288 | tf_op jit(solution)/shard_map/psum | solution.py:77
  906.0 1.2 multiply_reduce_fusion
  907.3 100.4 %psum.62 = f32[2,1536]{1,0:T(2,128)S(1)} all-reduce(f32[2,1536]{1,0:T(2,128)S(1)} %pad_maximum_fusion.1), channel_id=1, replica_groups=mesh['dp'=8,'tm'=64] {'dp','tm'}, use_global_device_ids=true, to_apply=%region_53.54 | all-reduce | flops 3072 | bytes 24576 | tf_op jit(solution)/shard_map/psum | solution.py:83
  1007.8 2.3 fusion.67
  1010.1 1.2 fusion.66
  1016.8 0.9 copy.78
  1017.7 1.4 dynamic-slice
  1019.0 1.3 dynamic-slice_add_fusion
  1020.4 475.1 %all-reduce.4.cloned.1.call-done = f32[64,6,128]{2,1,0:T(8,128)} async-done(((f32[64,6,128]{2,1,0:T(8,128)}), f32[64,6,128]{2,1,0:T(8,128)}) %all-reduce.4.cloned.1.call-update) | async-done | bytes 196624
  1495.5 1.4 constant_dynamic-slice_fusion
  1496.9 32.0 %psum.63 = f32[32,24]{1,0:T(8,128)S(1)} all-reduce(f32[32,24]{1,0:T(8,128)S(1)} %slice.682), channel_id=1, replica_groups=mesh['dp'=8,'tm'=64] {'dp'}, use_global_device_ids=true, to_apply=%region_86.87 | all-reduce | flops 768 | bytes 6144 | tf_op jit(solution)/shard_map/psum | solution.py:119
  (330 shorter events, 16.0 us)
Async XLA Ops:
  7.2 177.8 %copy-start = (bf16[1,128,1536]{2,1,0:T(8,128)(2,1)S(1)}, bf16[1,128,1536]{2,1,0:T(8,128)(2,1)}, u32[]{:S(2)}) copy-start(bf16[1,128,1536]{2,1,0:T(8,128)(2,1)} %param.9) | copy-start | bytes 1179652
  7.2 177.7 %copy-start.2 = (bf16[1,128,1536]{2,1,0:T(8,128)(2,1)S(1)}, bf16[1,128,1536]{2,1,0:T(8,128)(2,1)}, u32[]{:S(2)}) copy-start(bf16[1,128,1536]{2,1,0:T(8,128)(2,1)} %param.8) | copy-start | bytes 1179652
  7.2 177.7 %all-gather.2.cloned.1.call-start = ((), (), s32[]{:S(2)}) async-start(), calls=%async_computation | async-start | bytes 9584640 | tf_op jit(solution)/shard_map/all_gather | solution.py:54
  7.9 1487.5 %all-reduce.4.cloned.1.call-start = ((), (), s32[]{:S(2)}) async-start(), calls=%async_computation.1 | async-start | bytes 524288
  9.9 182.0 %copy-start.22 = (f32[128]{0:T(128)}, f32[128]{0:T(128)S(1)}, u32[]{:S(2)}) copy-start(f32[128]{0:T(128)S(1)} %fusion.133) | copy-start | bytes 1540
  10.5 181.3 %copy-start.42 = (f32[128]{0:T(128)}, f32[128]{0:T(128)S(1)}, u32[]{:S(2)}) copy-start(f32[128]{0:T(128)S(1)} %broadcast_select_fusion.1) | copy-start | bytes 1540
  13.7 178.2 %copy-start.46 = (f32[128]{0:T(128)}, f32[128]{0:T(128)S(1)}, u32[]{:S(2)}) copy-start(f32[128]{0:T(128)S(1)} %broadcast_multiply_fusion.3) | copy-start | bytes 1540
  16.3 175.5 %copy-start.44 = (f32[128]{0:T(128)}, f32[128]{0:T(128)S(1)}, u32[]{:S(2)}) copy-start(f32[128]{0:T(128)S(1)} %get-tuple-element.134) | copy-start | bytes 1540
  191.9 5.7 copy-start.49
  192.1 7.4 collective-permute-start
  194.3 5.3 collective-permute-start.1
  197.6 6.7 copy-start.8
  199.7 212.3 %copy-start.7 = (f32[1536]{0:T(1024)S(1)}, f32[1536]{0:T(1024)}, u32[]{:S(2)}) copy-start(f32[1536]{0:T(1024)} %param.13) | copy-start | bytes 18436
  520.8 2.3 copy-start.36
  520.8 2.5 copy-start.35
  520.8 2.7 copy-start.34
  520.8 2.8 copy-start.33
  520.8 3.0 copy-start.32
  520.9 3.1 copy-start.31
  520.9 3.3 copy-start.30
  520.9 3.4 copy-start.29
  520.9 3.6 copy-start.28
  520.9 3.7 copy-start.27
  522.1 2.7 copy-start.26
  522.1 2.9 copy-start.25
  522.6 8.0 copy-start.24
  522.7 11.2 copy-start.5
  525.6 8.6 copy-start.9
  525.6 8.6 copy-start.10
  525.6 8.6 copy-start.11
  525.6 8.6 copy-start.13
  525.6 8.6 copy-start.15
  525.6 8.6 copy-start.17
  525.6 8.6 copy-start.19
  525.6 8.6 copy-start.23
  527.2 3.6 collective-permute-start.2
  528.9 5.0 collective-permute-start.3
  534.0 3.8 slice-start
  534.2 3.6 slice-start.1
  534.2 3.6 slice-start.2
  683.9 4.9 copy-start.12
  683.9 4.9 copy-start.14
  683.9 4.9 copy-start.16
  683.9 4.9 copy-start.18
  683.9 4.9 copy-start.20
  684.2 2.8 collective-permute-start.4
  685.5 3.1 collective-permute-start.5
  688.8 217.2 %copy-start.6 = (bf16[1,128,1536]{2,1,0:T(8,128)(2,1)S(1)}, bf16[1,128,1536]{2,1,0:T(8,128)(2,1)}, u32[]{:S(2)}) copy-start(bf16[1,128,1536]{2,1,0:T(8,128)(2,1)} %param.10) | copy-start | bytes 1179652
  (13 other events, 18.4 us)
Sparse Core Ops, SparseCore 0:
  11.3 173.5 all-gather.1
  1017.8 477.6 all-reduce.3
where the time goes:
time: 1540 us
  blocking collectives  785 us (51%)
  waiting for transfers between devices  649 us (42%)
  other arithmetic  38 us (2%)
  local copies, waits for them, and re-layouts  21.8 us (1%)
  between operations  17.9 us (1%)
    unnamed x3, waiting for transfers between devices  476 us
    psum x2, blocking collectives, on_device(): lax.psum(jnp.sum(live * conv_out, axis=0), everywhere) / live_count  219 us
    psum x2, blocking collectives, on_device(): lax.psum(jnp.stack([jnp.sum(grad_pre * scaled, axis=0), jnp.sum(grad_pre,...  201 us
    psum x2, blocking collectives, on_device(): lax.psum(jnp.sum(live * centred * centred, axis=0), everywhere) / live_count  199 us
    all_gather x1, waiting for transfers between devices, on_device(): weight_full = lax.all_gather(in_weight, 'tm', axis=0, tiled=True)  169 us
    psum x1, blocking collectives, on_device(): square_total = lax.psum(jnp.sum(direction * direction), 'tm')  134 us
    psum x1, blocking collectives, on_device(): kernel_total = lax.psum(kernel_total, 'dp').reshape(-1)[:tap_count * width]  32 us
  transfers between devices with their start and end apart: 8, of which 4 were waited for; matrix products, arithmetic and copies ran while one was open for 1% of the time, Pallas kernels for 0%

commit v1 on v0

--- a/solution.py
+++ b/solution.py
@@ -80,8 +80,12 @@
         pre_act = bn_gain * scaled + bn_shift
         pre_sigmoid = jax.nn.sigmoid(pre_act)
         grad_pre = upstream * pre_sigmoid * (1.0 + pre_act * (1.0 - pre_sigmoid))
-        both = lax.psum(
-            jnp.stack([jnp.sum(grad_pre * scaled, axis=0), jnp.sum(grad_pre, axis=0)]), everywhere
+        both = jnp.sum(
+            lax.all_gather(
+                jnp.stack([jnp.sum(grad_pre * scaled, axis=0), jnp.sum(grad_pre, axis=0)]),
+                everywhere,
+            ),
+            axis=0,
         )
         norm_part = norm_part + both
         grad_conv = (

time: 1540 us -> 2970 us (1.93)
  waiting for transfers between devices: 649 us -> 2270 us
  blocking collectives: 785 us -> 576 us
    all_gather x0 -> x2, waiting for transfers between devices: none -> 1630 us  [on_device(): lax.all_gather(jnp.stack([jnp.sum(grad_pre * scaled, axis=0), jnp.sum(gra...]
    psum x2 -> x0, blocking collectives: 201 us -> none  [on_device(): lax.psum(jnp.stack([jnp.sum(grad_pre * scaled, axis=0), jnp.sum(grad_pre,...]
    unnamed x3 -> x5, waiting for transfers between devices: 476 us -> 476 us
  transfers between devices with their start and end apart: 8 -> 10, of which waited for: 4 -> 5; matrix products, arithmetic and copies ran while one was open for 1% -> 1% of each run, Pallas kernels for 0% -> 0%
where the time goes in v1:
time: 2970 us
  waiting for transfers between devices  2270 us (76%)
  blocking collectives  576 us (19%)
  other arithmetic  54.1 us (2%)
    all_gather x2, waiting for transfers between devices, on_device(): lax.all_gather(jnp.stack([jnp.sum(grad_pre * scaled, axis=0), jnp.sum(gra...  1630 us
    unnamed x5, waiting for transfers between devices  476 us
    psum x2, blocking collectives, on_device(): lax.psum(jnp.sum(live * conv_out, axis=0), everywhere) / live_count  212 us
    psum x2, blocking collectives, on_device(): lax.psum(jnp.sum(live * centred * centred, axis=0), everywhere) / live_count  201 us
    all_gather x1, waiting for transfers between devices, on_device(): weight_full = lax.all_gather(in_weight, 'tm', axis=0, tiled=True)  168 us
    psum x1, blocking collectives, on_device(): square_total = lax.psum(jnp.sum(direction * direction), 'tm')  132 us
  transfers between devices with their start and end apart: 10, of which 5 were waited for; matrix products, arithmetic and copies ran while one was open for 1% of the time, Pallas kernels for 0%

profile of v1, /device:TPU:2, one launch (start us, length us, event | category | flops | bytes accessed | tf_op | source)
XLA Modules:
  0.0 2971.6 jit_solution(10412478106846725645)
XLA Ops:
  7.9 1.2 dynamic_slice.7
  10.5 1.8 slice_reduce_fusion.34
  12.5 1.4 fusion.121
  13.9 1.4 multiply_reduce_fusion.7
  15.4 1.2 broadcast_select_fusion
  16.5 168.4 %all-gather.8.cloned.1.call-done = bf16[3072,1536]{1,0:T(8,128)(2,1)} async-done(((bf16[48,1536]{1,0:T(8,128)(2,1)}), bf16[3072,1536]{1,0:T(8,128)(2,1)}) %all-gather.8.cloned.1.call-update) | async-done | bytes 9437200 | tf_op jit(solution)/shard_map/all_gather | solution.py:54
  184.9 7.2 fusion.122
  192.4 1.3 collective-permute-start.1
  193.7 3.0 collective-permute-start
  196.7 2.1 slice_reduce_fusion.33
  200.4 4.5 multiply_reduce_fusion.6
  204.9 104.2 %psum.42 = f32[1536]{0:T(1024)} all-reduce(f32[1536]{0:T(1024)} %get-tuple-element.124), channel_id=1, replica_groups=mesh['dp'=8,'tm'=64] {'dp','tm'}, use_global_device_ids=true, to_apply=%region_3.4 | all-reduce | flops 1536 | bytes 12288 | tf_op jit(solution)/shard_map/psum | solution.py:75
  309.8 1.4 fusion.4
  311.2 99.4 %psum.43 = f32[1536]{0:T(1024)} all-reduce(f32[1536]{0:T(1024)} %fusion.4), channel_id=1, replica_groups=mesh['dp'=8,'tm'=64] {'dp','tm'}, use_global_device_ids=true, to_apply=%region_6.7 | all-reduce | flops 1536 | bytes 12288 | tf_op jit(solution)/shard_map/psum | solution.py:77
  411.9 2.4 multiply_reduce_fusion.5
  415.0 817.2 %all-gather.10.cloned.1.call-done = f32[512,2,1536]{2,1,0:T(2,128)} async-done(((f32[1,2,1536]{2,1,0:T(2,128)}), f32[512,2,1536]{2,1,0:T(2,128)}) %all-gather.10.cloned.1.call-update) | async-done | bytes 6291472 | tf_op jit(solution)/shard_map/all_gather | solution.py:84
  1232.1 5.1 reduce_sum.727
  1237.2 0.8 slice_reduce_fusion.3
  1238.0 4.0 fusion.36
  1242.1 0.7 copy-done.2
  1242.8 1.3 collective-permute-start.3
  1244.1 3.2 collective-permute-start.2
  1248.1 1.3 maximum_convert_fusion.1
  1249.7 4.2 fusion
  1254.2 1.5 fusion.134
  1255.8 1.2 multiply_reduce_fusion.3
  1256.9 131.7 %psum.44 = f32[]{:T(128)} all-reduce(f32[]{:T(128)} %get-tuple-element.119), channel_id=1, replica_groups=mesh['dp'=8,'tm'=64] {'tm'}, use_global_device_ids=true, to_apply=%region_13.14 | all-reduce | flops 1 | bytes 8 | tf_op jit(solution)/shard_map/psum | solution.py:113
  1389.3 1.1 fusion.136
  1391.0 6.8 fusion.124
  1398.1 1.3 collective-permute-start.5
  1399.4 3.0 collective-permute-start.4
  1402.5 0.9 collective-permute-done.4
  1403.8 3.7 multiply_reduce_fusion.1
  1407.5 107.6 %psum.45 = f32[1536]{0:T(1024)} all-reduce(f32[1536]{0:T(1024)} %get-tuple-element.114), channel_id=1, replica_groups=mesh['dp'=8,'tm'=64] {'dp','tm'}, use_global_device_ids=true, to_apply=%region_48.49 | all-reduce | flops 1536 | bytes 12288 | tf_op jit(solution)/shard_map/psum | solution.py:75
  1515.8 1.4 fusion.5
  1517.2 101.4 %psum.46 = f32[1536]{0:T(1024)} all-reduce(f32[1536]{0:T(1024)} %fusion.5), channel_id=1, replica_groups=mesh['dp'=8,'tm'=64] {'dp','tm'}, use_global_device_ids=true, to_apply=%region_50.51 | all-reduce | flops 1536 | bytes 12288 | tf_op jit(solution)/shard_map/psum | solution.py:77
  1619.3 2.1 multiply_reduce_fusion
  1622.5 1.2 fusion.35
  1629.2 809.0 %all-gather.12.cloned.1.call-done = f32[512,2,1536]{2,1,0:T(2,128)} async-done(((f32[1,2,1536]{2,1,0:T(2,128)}), f32[512,2,1536]{2,1,0:T(2,128)}) %all-gather.12.cloned.1.call-update) | async-done | bytes 6291472 | tf_op jit(solution)/shard_map/all_gather | solution.py:84
  2438.1 4.5 reduce_sum.768
  2442.7 2.3 fusion.67
  2445.1 1.2 fusion.66
  2451.7 0.9 copy.78
  2452.6 1.4 dynamic-slice
  2454.0 1.3 dynamic-slice_add_fusion
  2455.3 475.6 %all-reduce.4.cloned.1.call-done = f32[64,6,128]{2,1,0:T(8,128)} async-done(((f32[64,6,128]{2,1,0:T(8,128)}), f32[64,6,128]{2,1,0:T(8,128)}) %all-reduce.4.cloned.1.call-update) | async-done | bytes 196624
  2930.9 1.4 constant_dynamic-slice_fusion
  2932.4 32.0 %psum.47 = f32[32,24]{1,0:T(8,128)S(1)} all-reduce(f32[32,24]{1,0:T(8,128)S(1)} %slice.682), channel_id=1, replica_groups=mesh['dp'=8,'tm'=64] {'dp'}, use_global_device_ids=true, to_apply=%region_86.87 | all-reduce | flops 768 | bytes 6144 | tf_op jit(solution)/shard_map/psum | solution.py:123
  (422 shorter events, 20.1 us)
Async XLA Ops:
  7.2 177.7 %all-gather.8.cloned.1.call-start = ((), (), s32[]{:S(2)}) async-start(), calls=%async_computation | async-start | bytes 9584640 | tf_op jit(solution)/shard_map/all_gather | solution.py:54
  7.9 1224.2 %all-gather.10.cloned.1.call-start = ((), (), s32[]{:S(2)}) async-start(), calls=%async_computation.1 | async-start | bytes 6303744 | tf_op jit(solution)/shard_map/all_gather | solution.py:84
  9.8 182.2 %copy-start.85 = (f32[128]{0:T(128)}, f32[128]{0:T(128)S(1)}, u32[]{:S(2)}) copy-start(f32[128]{0:T(128)S(1)} %broadcast_select_fusion.1) | copy-start | bytes 1540
  10.5 181.6 %copy-start.64 = (f32[128]{0:T(128)}, f32[128]{0:T(128)S(1)}, u32[]{:S(2)}) copy-start(f32[128]{0:T(128)S(1)} %fusion.133) | copy-start | bytes 1540
  12.3 1237.0 %copy-start.7 = (f32[1536]{0:T(1024)}, f32[1536]{0:T(1024)S(1)}, u32[]{:S(2)}) copy-start(f32[1536]{0:T(1024)S(1)} %get-tuple-element.78) | copy-start | bytes 18436
  12.4 1237.0 %copy-start.9 = (f32[1536]{0:T(1024)}, f32[1536]{0:T(1024)S(1)}, u32[]{:S(2)}) copy-start(f32[1536]{0:T(1024)S(1)} %get-tuple-element.79) | copy-start | bytes 18436
  12.4 1237.0 %copy-start.11 = (f32[1536]{0:T(1024)}, f32[1536]{0:T(1024)S(1)}, u32[]{:S(2)}) copy-start(f32[1536]{0:T(1024)S(1)} %get-tuple-element.80) | copy-start | bytes 18436
  12.4 1237.0 %copy-start.13 = (f32[1536]{0:T(1024)}, f32[1536]{0:T(1024)S(1)}, u32[]{:S(2)}) copy-start(f32[1536]{0:T(1024)S(1)} %get-tuple-element.81) | copy-start | bytes 18436
  12.4 1237.0 %copy-start.15 = (f32[1536]{0:T(1024)}, f32[1536]{0:T(1024)S(1)}, u32[]{:S(2)}) copy-start(f32[1536]{0:T(1024)S(1)} %get-tuple-element.82) | copy-start | bytes 18436
  12.4 1237.0 %copy-start.17 = (f32[1536]{0:T(1024)}, f32[1536]{0:T(1024)S(1)}, u32[]{:S(2)}) copy-start(f32[1536]{0:T(1024)S(1)} %get-tuple-element.83) | copy-start | bytes 18436
  12.4 1237.0 %copy-start.19 = (f32[1536]{0:T(1024)}, f32[1536]{0:T(1024)S(1)}, u32[]{:S(2)}) copy-start(f32[1536]{0:T(1024)S(1)} %get-tuple-element.84) | copy-start | bytes 18436
  12.4 1237.0 %copy-start.21 = (f32[1536]{0:T(1024)}, f32[1536]{0:T(1024)S(1)}, u32[]{:S(2)}) copy-start(f32[1536]{0:T(1024)S(1)} %get-tuple-element.85) | copy-start | bytes 18436
  12.4 1237.0 %copy-start.23 = (f32[1536]{0:T(1024)}, f32[1536]{0:T(1024)S(1)}, u32[]{:S(2)}) copy-start(f32[1536]{0:T(1024)S(1)} %get-tuple-element.86) | copy-start | bytes 18436
  12.4 1237.0 %copy-start.25 = (f32[1536]{0:T(1024)}, f32[1536]{0:T(1024)S(1)}, u32[]{:S(2)}) copy-start(f32[1536]{0:T(1024)S(1)} %get-tuple-element.87) | copy-start | bytes 18436
  12.4 1237.0 %copy-start.27 = (f32[1536]{0:T(1024)}, f32[1536]{0:T(1024)S(1)}, u32[]{:S(2)}) copy-start(f32[1536]{0:T(1024)S(1)} %get-tuple-element.88) | copy-start | bytes 18436
  12.5 1237.0 %copy-start.29 = (f32[1536]{0:T(1024)}, f32[1536]{0:T(1024)S(1)}, u32[]{:S(2)}) copy-start(f32[1536]{0:T(1024)S(1)} %get-tuple-element.89) | copy-start | bytes 18436
  12.5 1237.0 %copy-start.31 = (f32[1536]{0:T(1024)}, f32[1536]{0:T(1024)S(1)}, u32[]{:S(2)}) copy-start(f32[1536]{0:T(1024)S(1)} %get-tuple-element.90) | copy-start | bytes 18436
  12.5 1237.0 %copy-start.33 = (f32[1536]{0:T(1024)}, f32[1536]{0:T(1024)S(1)}, u32[]{:S(2)}) copy-start(f32[1536]{0:T(1024)S(1)} %get-tuple-element.91) | copy-start | bytes 18436
  12.5 1237.0 %copy-start.35 = (f32[1536]{0:T(1024)}, f32[1536]{0:T(1024)S(1)}, u32[]{:S(2)}) copy-start(f32[1536]{0:T(1024)S(1)} %get-tuple-element.92) | copy-start | bytes 18436
  12.5 1237.0 %copy-start.37 = (f32[1536]{0:T(1024)}, f32[1536]{0:T(1024)S(1)}, u32[]{:S(2)}) copy-start(f32[1536]{0:T(1024)S(1)} %get-tuple-element.93) | copy-start | bytes 18436
  12.5 1237.0 %copy-start.39 = (f32[1536]{0:T(1024)}, f32[1536]{0:T(1024)S(1)}, u32[]{:S(2)}) copy-start(f32[1536]{0:T(1024)S(1)} %get-tuple-element.94) | copy-start | bytes 18436
  12.5 1237.0 %copy-start.41 = (f32[1536]{0:T(1024)}, f32[1536]{0:T(1024)S(1)}, u32[]{:S(2)}) copy-start(f32[1536]{0:T(1024)S(1)} %get-tuple-element.95) | copy-start | bytes 18436
  13.9 178.2 %copy-start.89 = (f32[128]{0:T(128)}, f32[128]{0:T(128)S(1)}, u32[]{:S(2)}) copy-start(f32[128]{0:T(128)S(1)} %broadcast_multiply_fusion.3) | copy-start | bytes 1540
  16.5 175.8 %copy-start.87 = (f32[128]{0:T(128)}, f32[128]{0:T(128)S(1)}, u32[]{:S(2)}) copy-start(f32[128]{0:T(128)S(1)} %get-tuple-element.134) | copy-start | bytes 1540
  184.9 14.0 copy-start.92
  192.4 7.8 collective-permute-start.1
  193.7 6.5 collective-permute-start
  198.9 1050.7 %copy-start.43 = (f32[1536]{0:T(1024)}, f32[1536]{0:T(1024)S(1)}, u32[]{:S(2)}) copy-start(f32[1536]{0:T(1024)S(1)} %get-tuple-element.96) | copy-start | bytes 18436
  198.9 1050.7 %copy-start.45 = (f32[1536]{0:T(1024)}, f32[1536]{0:T(1024)S(1)}, u32[]{:S(2)}) copy-start(f32[1536]{0:T(1024)S(1)} %get-tuple-element.97) | copy-start | bytes 18436
  198.9 1050.7 %copy-start.47 = (f32[1536]{0:T(1024)}, f32[1536]{0:T(1024)S(1)}, u32[]{:S(2)}) copy-start(f32[1536]{0:T(1024)S(1)} %get-tuple-element.98) | copy-start | bytes 18436
  198.9 1050.7 %copy-start.49 = (f32[1536]{0:T(1024)}, f32[1536]{0:T(1024)S(1)}, u32[]{:S(2)}) copy-start(f32[1536]{0:T(1024)S(1)} %get-tuple-element.99) | copy-start | bytes 18436
  198.9 1050.7 %copy-start.51 = (f32[1536]{0:T(1024)}, f32[1536]{0:T(1024)S(1)}, u32[]{:S(2)}) copy-start(f32[1536]{0:T(1024)S(1)} %get-tuple-element.100) | copy-start | bytes 18436
  200.3 211.5 %copy-start.6 = (f32[1536]{0:T(1024)S(1)}, f32[1536]{0:T(1024)}, u32[]{:S(2)}) copy-start(f32[1536]{0:T(1024)} %param.13) | copy-start | bytes 18436
  414.9 2023.2 %all-gather.12.cloned.1.call-start = ((), (), s32[]{:S(2)}) async-start(), calls=%async_computation.2 | async-start | bytes 6303744 | tf_op jit(solution)/shard_map/all_gather | solution.py:84
  1242.8 5.2 collective-permute-start.3
  1244.1 3.9 collective-permute-start.2
  1390.7 12.7 copy-start.8
  1390.7 12.7 copy-start.10
  1390.7 12.7 copy-start.12
  1390.7 12.7 copy-start.14
  1398.1 4.3 collective-permute-start.5
  1399.4 3.9 collective-permute-start.4
  1403.7 215.6 %copy-start.5 = (bf16[1,128,1536]{2,1,0:T(8,128)(2,1)S(1)}, bf16[1,128,1536]{2,1,0:T(8,128)(2,1)}, u32[]{:S(2)}) copy-start(bf16[1,128,1536]{2,1,0:T(8,128)(2,1)} %param.10) | copy-start | bytes 1179652
  1403.8 218.8 %copy-start.3 = (bf16[128,1536]{1,0:T(8,128)(2,1)S(1)}, bf16[128,1536]{1,0:T(8,128)(2,1)}, u32[]{:S(2)}) copy-start(bf16[128,1536]{1,0:T(8,128)(2,1)} %copy-done.2) | copy-start | bytes 1179652
  1622.2 1308.7 %all-reduce.4.cloned.1.call-start = ((), (), s32[]{:S(2)}) async-start(), calls=%async_computation.3 | async-start | bytes 524288
  1623.7 819.0 %copy-start.4 = (f32[128,1536]{1,0:T(8,128)S(1)}, f32[128,1536]{1,0:T(8,128)}, u32[]{:S(2)}) copy-start(f32[128,1536]{1,0:T(8,128)} %get-tuple-element.113) | copy-start | bytes 2359300
  1623.7 819.0 %copy-start.62 = (f32[1536]{0:T(1024)S(1)}, f32[1536]{0:T(1024)}, u32[]{:S(2)}) copy-start(f32[1536]{0:T(1024)} %copy-done.61) | copy-start | bytes 18436
  1623.7 819.0 %copy-start.66 = (f32[128]{0:T(128)S(1)}, f32[128]{0:T(128)}, u32[]{:S(2)}) copy-start(f32[128]{0:T(128)} %copy-done.64) | copy-start | bytes 1540
  (58 other events, 457.6 us)
Sparse Core Ops, SparseCore 0:
  11.3 173.5 all-gather.7
  415.0 817.0 all-gather.9
  1622.3 815.7 all-gather.11
  2452.7 478.1 all-reduce.3
